TPU v7x, 256 devices: a whole 4x4x8 slice. The times are simulated.
256 devices in a mesh: seq: 16 (over z, core), head: 16 (over x, y).
Axes of the slice: x: 4, y: 4, z: 8, core: 2. Of those that a mesh axis runs over, the one named last changes fastest.
Arguments:
- features: bfloat16 [65536, 8192], P(('seq', 'head')), may hold values from -6 to 6
- step_size: float32 [65536, 128], P(('seq', 'head')), may hold values from 0.01 to 0.08
- log_decay: float32 [65536, 128], P(('seq', 'head')), may hold values from -0.6 to 0
- inject: bfloat16 [65536, 1024], P(('seq', 'head')), may hold values from -1.5 to 1.5
- readout: bfloat16 [65536, 1024], P(('seq', 'head')), may hold values from -1.5 to 1.5
- skip_gain: float32 [128], replicated, may hold values from 0.5 to 1.5
Outputs:
- mixer_out: bfloat16 [65536, 8192], P(('seq', 'head'))
All inputs are finite; a program needn't handle non-finite values.
Results may differ from a plain program's by a relative error of at most 0.02.
Values may be sent and summed in bfloat16 or wider, within the bound.
No kernel may reach another device: no remote copies, remote signals or barrier semaphores. Data moves between devices by JAX's collectives and lax.ppermute only.
A program may use at most 128 MiB of HBM per device.

v0:
```python
import jax
import jax.numpy as jnp
from jax import lax
from jax.sharding import PartitionSpec as P

HEAD_DIM = 64
STATE = 128
GROUPS = 8
SPAN = 512


def entering_2(x, axis, join, neutral):
    place = lax.axis_index(axis)
    gathered = jax.tree.map(
        lambda a, kind: lax.all_gather(a.astype(kind), axis), x, (jnp.bfloat16, jnp.bfloat16)
    )
    state = jax.tree.map(lambda a, e: jnp.zeros_like(a) + jnp.asarray(e, a.dtype), x, neutral)

    def one(step, state):
        return join(
            state,
            jax.tree.map(
                lambda a, own: lax.dynamic_index_in_dim(a, step, 0, False).astype(own.dtype),
                gathered,
                x,
            ),
        )

    return lax.fori_loop(0, place, one, state)


def shards(features, step_size, log_decay, inject, readout, skip_gain):
    head_ways = lax.axis_size("head")
    head_index = lax.axis_index("head")
    heads_all = step_size.shape[1]
    local_heads = heads_all // head_ways
    group_heads = heads_all // GROUPS
    local_groups = max(1, local_heads // group_heads)
    per_group = local_heads // local_groups
    regrouped = lax.all_to_all(features, "head", split_axis=1, concat_axis=0, tiled=True)
    steps_local, decay_local = (
        lax.all_to_all(
            step_size.astype(jnp.bfloat16), "head", split_axis=1, concat_axis=0, tiled=True
        ).astype(step_size.dtype),
        lax.all_to_all(
            log_decay.astype(jnp.bfloat16), "head", split_axis=1, concat_axis=0, tiled=True
        ).astype(log_decay.dtype),
    )
    inject_all, readout_all = (
        lax.all_gather(inject, "head", axis=0, tiled=True),
        lax.all_gather(readout, "head", axis=0, tiled=True),
    )
    first_col = head_index * local_heads // group_heads * STATE
    inject_mine = lax.dynamic_slice_in_dim(inject_all, first_col, local_groups * STATE, 1)
    readout_mine = lax.dynamic_slice_in_dim(readout_all, first_col, local_groups * STATE, 1)
    seq_rows = regrouped.shape[0]
    spans = seq_rows // SPAN
    drive = (
        regrouped.reshape(seq_rows, local_heads, HEAD_DIM).astype(jnp.float32)
        * steps_local[:, :, None]
    ).astype(jnp.bfloat16)
    drive_q = drive.reshape(spans, SPAN, local_groups, per_group, HEAD_DIM)
    cum_q = jnp.cumsum(decay_local.reshape(spans, SPAN, local_heads), axis=1)
    inject_q = inject_mine.reshape(spans, SPAN, local_groups, STATE)
    readout_q = readout_mine.reshape(spans, SPAN, local_groups, STATE)
    row_ids = lax.broadcasted_iota(jnp.int32, (SPAN, SPAN), 0)
    col_ids = lax.broadcasted_iota(jnp.int32, (SPAN, SPAN), 1)
    lower_mask = row_ids >= col_ids

    def span_terms(pieces):
        read_c, inject_c, drive_c, cum_c = pieces
        intersection = jnp.einsum(
            "ign,jgn->gij", read_c, inject_c, preferred_element_type=jnp.float32
        )
        cum_heads = cum_c.T
        log_gap = cum_heads[:, :, None] - cum_heads[:, None, :]
        decays = jnp.where(lower_mask, jnp.exp(jnp.where(lower_mask, log_gap, 0.0)), 0.0)
        weights = (
            decays.reshape(local_groups, per_group, SPAN, SPAN) * intersection[:, None]
        ).astype(jnp.bfloat16)
        inner_out = jnp.einsum(
            "ghij,jghp->ighp", weights, drive_c, preferred_element_type=jnp.float32
        )
        tail_decay = jnp.exp(cum_heads[:, -1:] - cum_heads)
        scaled = (
            drive_c.astype(jnp.float32)
            * tail_decay.T.reshape(SPAN, local_groups, per_group)[..., None]
        ).astype(jnp.bfloat16)
        summary = jnp.einsum("jghp,jgn->ghpn", scaled, inject_c, preferred_element_type=jnp.float32)
        return (inner_out, summary.reshape(local_heads, HEAD_DIM, STATE))

    inner_out, summary = lax.map(span_terms, (readout_q, inject_q, drive_q, cum_q))
    totals = cum_q[:, -1, :]

    def advance(carried, pieces):
        block_total, summary_c = pieces
        updated = carried * jnp.exp(block_total)[:, None, None] + summary_c
        return (updated, carried)

    zero_state = jnp.zeros((local_heads, HEAD_DIM, STATE), jnp.float32)
    end_state, entering = lax.scan(advance, zero_state, (totals, summary))
    dev_total = jnp.sum(totals, axis=0)

    def combine(earlier, following):
        return (
            earlier[0] + following[0],
            earlier[1] * jnp.exp(following[0])[:, None, None] + following[1],
        )

    identity = (jnp.zeros((local_heads,), jnp.float32), zero_state)
    scanned = entering_2((dev_total, end_state), "seq", combine, identity)
    incoming = scanned[1]
    before = jnp.cumsum(totals, axis=0) - totals
    states = entering + jnp.exp(before)[:, :, None, None] * incoming[None]
    held = states.astype(jnp.bfloat16).reshape(spans, local_groups, per_group, HEAD_DIM, STATE)
    outer_out = jnp.einsum("cign,cghpn->cighp", readout_q, held, preferred_element_type=jnp.float32)
    outer_out = outer_out * jnp.exp(cum_q).reshape(spans, SPAN, local_groups, per_group)[..., None]
    skip_local = lax.dynamic_slice_in_dim(skip_gain, head_index * local_heads, local_heads)
    plain = regrouped.reshape(spans, SPAN, local_groups, per_group, HEAD_DIM).astype(jnp.float32)
    total_out = (
        inner_out + outer_out + skip_local.reshape(local_groups, per_group)[:, :, None] * plain
    )
    mixed_rows = total_out.astype(jnp.bfloat16).reshape(seq_rows, local_heads * HEAD_DIM)
    return lax.all_to_all(mixed_rows, "head", split_axis=0, concat_axis=1, tiled=True)


def solution(mesh):
    placed = (
        P(("seq", "head"), None),
        P(("seq", "head"), None),
        P(("seq", "head"), None),
        P(("seq", "head"), None),
        P(("seq", "head"), None),
        P(),
    )
    return jax.shard_map(
        shards, mesh=mesh, in_specs=placed, out_specs=P(("seq", "head"), None), check_vma=False
    )
```

profile of v0, /device:TPU:225, one launch (start us, length us, event | category | flops | bytes accessed | tf_op | source)
XLA Modules:
  0.0 422.0 jit_solution(15952692852257553255)
XLA Ops:
  9.6 6.8 %all-to-all-start.2 = ((bf16[256,16,8]{0,2,1:T(8,128)(2,1)}), bf16[256,16,8]{0,2,1:T(8,128)(2,1)S(1)}, u32[]{:S(2)}, u32[]{:S(2)}) async-start(bf16[256,16,8]{0,2,1:T(8,128)(2,1)} %bitcast.102), calls=%async_computation.2 | async-start | bytes 131072 | tf_op jit(solution)/shard_map/all_to_all | solution.py:45
  18.0 4.9 %all-to-all-done.2 = bf16[256,16,8]{0,2,1:T(8,128)(2,1)S(1)} async-done(((bf16[256,16,8]{0,2,1:T(8,128)(2,1)}), bf16[256,16,8]{0,2,1:T(8,128)(2,1)S(1)}, u32[]{:S(2)}, u32[]{:S(2)}) %all-to-all-start.2) | async-done | bytes 65568 | tf_op jit(solution)/shard_map/all_to_all | solution.py:45
  26.4 6.4 %copy.78 = bf16[256,8192]{0,1:T(8,128)(2,1)} copy(bf16[256,8192]{1,0:T(8,128)(2,1)} %param.12) | data formatting | bytes 8388608 | tf_op args[0]
  33.2 6.3 %all-to-all-start = ((bf16[256,16,512]{0,2,1:T(8,128)(2,1)}), bf16[256,16,512]{0,2,1:T(8,128)(2,1)}, u32[]{:S(2)}, u32[]{:S(2)}) async-start(bf16[256,16,512]{0,2,1:T(8,128)(2,1)} %bitcast.134), calls=%async_computation | async-start | bytes 8388608 | tf_op jit(solution)/shard_map/all_to_all | solution.py:40
  39.6 9.0 %reduce-window.6 = f32[8,8,4,128]{3,1,2,0:T(8,128)S(1)} reduce-window(f32[8,8,4,128]{3,1,2,0:T(8,128)S(1)} %bitcast.139, f32[]{:T(128)} %constant.75.clone.1), window={size=1x1x1x128 pad=0_0x0_0x0_0x127_0}, to_apply=%region_0.1 | reduce-window | flops 4161536 | bytes 262148 | tf_op jit(solution)/shard_map/reduce-window
  49.6 65.2 %all-to-all-done = bf16[256,16,512]{0,2,1:T(8,128)(2,1)} async-done(((bf16[256,16,512]{0,2,1:T(8,128)(2,1)}), bf16[256,16,512]{0,2,1:T(8,128)(2,1)}, u32[]{:S(2)}, u32[]{:S(2)}) %all-to-all-start) | async-done | bytes 4194336 | tf_op jit(solution)/shard_map/all_to_all | solution.py:40
  117.9 8.1 %copy.79 = f32[16,256,512]{1,0,2:T(8,128)} copy(f32[16,256,512]{1,2,0:T(8,128)S(1)} %convert_bitcast_fusion) | data formatting | bytes 16777216 | tf_op jit(solution)/shard_map/convert_element_type | solution.py:59
  125.9 9.8 %reshape.178 = f32[8,512,1,8,64]{1,0,4,3,2:T(8,128)} reshape(f32[16,256,512]{1,0,2:T(8,128)} %copy.79) | data formatting | bytes 16777216 | tf_op jit(solution)/shard_map/convert_element_type | solution.py:59
  135.7 5.1 %multiply_convert_fusion.7 = bf16[8,512,1,8,64]{1,0,4,3,2:T(8,128)(2,1)S(1)} fusion(f32[8,512,1,8,64]{1,0,4,3,2:T(8,128)} %reshape.178, f32[8,512,8]{1,0,2:T(8,128)S(1)} %copy.81), kind=kLoop, calls=%fused_computation.43 | loop fusion | flops 4194304 | bytes 12713984 | tf_op jit(solution)/shard_map/convert_element_type | solution.py:61
  145.6 54.1 %all-gather.8.cloned.1.call-done = bf16[4096,1024]{1,0:T(8,128)(2,1)} async-done(((bf16[256,1024]{1,0:T(8,128)(2,1)}), bf16[4096,1024]{1,0:T(8,128)(2,1)}) %all-gather.8.cloned.1.call-update) | async-done | bytes 8388624 | tf_op jit(solution)/shard_map/all_gather | solution.py:50
  202.6 59.0 %while.40 = (s32[]{:T(128)}, f32[8,512,1,8,64]{1,4,3,2,0:T(8,128)}, f32[8,8,64,128]{3,2,1,0:T(8,128)}, bf16[8,512,1,8,64]{1,4,3,2,0:T(8,128)(2,1)}, f32[8,512,8]...) while((s32[]{:T(128)}, f32[8,512,1,8,64]{1,4,3,2,0:T(8,128)}, ...), condition=%wide.region_3.4_spmd.clone.clone, body=%wide.region_2.3_spmd.clone.clone.sunk | while | flops 414191616 | bytes 5492413 | solution.py:92
  203.0 4.7 %fusion.52 = f32[8,512,1,8,64]{1,4,3,2,0:T(8,128)} fusion(f32[8,512,1,8,64]{1,4,3,2,0:T(8,128)} %get-tuple-element.377, s32[]{:T(128)} %get-tuple-element.376, f32[512,512]{1,0:T(8,128)S(1)} %fusion.51, f32[8,512]{1,0:T(8,128)S(1)} %dynamic-slice_bitcast_fusion.2, pred[512,512]{1,0:T(8,128)(4,1)S(1)} %iota_compare_fusion.2, ...), kind=kOutput, calls=%fused_computation.12.clone.1 | convolution fusion | flops 278921216 | bytes 2917376 | tf_op jit(solution)/shard_map/while/body/eval_jaxpr/ghij,jghp->ighp/dot_general | solution.py:81
  217.7 4.7 %fusion.52 = f32[8,512,1,8,64]{1,4,3,2,0:T(8,128)} fusion(f32[8,512,1,8,64]{1,4,3,2,0:T(8,128)} %get-tuple-element.377, s32[]{:T(128)} %get-tuple-element.376, f32[512,512]{1,0:T(8,128)S(1)} %fusion.51, f32[8,512]{1,0:T(8,128)S(1)} %dynamic-slice_bitcast_fusion.2, pred[512,512]{1,0:T(8,128)(4,1)S(1)} %iota_compare_fusion.2, ...), kind=kOutput, calls=%fused_computation.12.clone.1 | convolution fusion | flops 278921216 | bytes 2917376 | tf_op jit(solution)/shard_map/while/body/eval_jaxpr/ghij,jghp->ighp/dot_general | solution.py:81
  225.1 4.7 %fusion.52 = f32[8,512,1,8,64]{1,4,3,2,0:T(8,128)} fusion(f32[8,512,1,8,64]{1,4,3,2,0:T(8,128)} %get-tuple-element.377, s32[]{:T(128)} %get-tuple-element.376, f32[512,512]{1,0:T(8,128)S(1)} %fusion.51, f32[8,512]{1,0:T(8,128)S(1)} %dynamic-slice_bitcast_fusion.2, pred[512,512]{1,0:T(8,128)(4,1)S(1)} %iota_compare_fusion.2, ...), kind=kOutput, calls=%fused_computation.12.clone.1 | convolution fusion | flops 278921216 | bytes 2917376 | tf_op jit(solution)/shard_map/while/body/eval_jaxpr/ghij,jghp->ighp/dot_general | solution.py:81
  232.5 4.7 %fusion.52 = f32[8,512,1,8,64]{1,4,3,2,0:T(8,128)} fusion(f32[8,512,1,8,64]{1,4,3,2,0:T(8,128)} %get-tuple-element.377, s32[]{:T(128)} %get-tuple-element.376, f32[512,512]{1,0:T(8,128)S(1)} %fusion.51, f32[8,512]{1,0:T(8,128)S(1)} %dynamic-slice_bitcast_fusion.2, pred[512,512]{1,0:T(8,128)(4,1)S(1)} %iota_compare_fusion.2, ...), kind=kOutput, calls=%fused_computation.12.clone.1 | convolution fusion | flops 278921216 | bytes 2917376 | tf_op jit(solution)/shard_map/while/body/eval_jaxpr/ghij,jghp->ighp/dot_general | solution.py:81
  247.2 4.7 %fusion.52 = f32[8,512,1,8,64]{1,4,3,2,0:T(8,128)} fusion(f32[8,512,1,8,64]{1,4,3,2,0:T(8,128)} %get-tuple-element.377, s32[]{:T(128)} %get-tuple-element.376, f32[512,512]{1,0:T(8,128)S(1)} %fusion.51, f32[8,512]{1,0:T(8,128)S(1)} %dynamic-slice_bitcast_fusion.2, pred[512,512]{1,0:T(8,128)(4,1)S(1)} %iota_compare_fusion.2, ...), kind=kOutput, calls=%fused_computation.12.clone.1 | convolution fusion | flops 278921216 | bytes 2917376 | tf_op jit(solution)/shard_map/while/body/eval_jaxpr/ghij,jghp->ighp/dot_general | solution.py:81
  261.9 8.9 %while.41 = (s32[]{:T(128)}, f32[8,64,128]{2,1,0:T(8,128)S(1)}, f32[8,8,64,128]{3,2,1,0:T(8,128)S(1)}, f32[8,8]{1,0:T(8,128)S(1)}, f32[8,8,64,128]{3,2,1,0:T(8,128)}, /*index=5*/s32[]{:T(128)}, s32[]{:T(128)}) while((s32[]{:T(128)}, f32[8,64,128]{2,1,0:T(8,128)S(1)}, f32[8,8,64,128]{3,2,1,0:T(8,128)S(1)}, f32[8,8]{1,0:T(8,128)S(1)}, ...), condition=%wide.region_5.6_spmd.clone, body=%wide.region_4.5_spmd.clone.sunk | while | flops 262147 | bytes 1310916 | solution.py:101
  273.2 23.8 %all-reduce = bf16[128]{0:T(256)(128)(2,1)S(1)} all-reduce(bf16[128]{0:T(256)(128)(2,1)S(1)} %dynamic-update-slice), channel_id=2, replica_groups=mesh['seq'=16,'head'=16] {'seq'}, use_global_device_ids=true, to_apply=%add | all-reduce | flops 128 | bytes 512
  297.1 12.5 %all-gather.10.cloned.1.call-done = bf16[128,64,128]{2,1,0:T(8,128)(2,1)} async-done(((bf16[8,64,128]{2,1,0:T(8,128)(2,1)}), bf16[128,64,128]{2,1,0:T(8,128)(2,1)}) %all-gather.10.cloned.1.call-update) | async-done | bytes 2097168 | tf_op jit(solution)/shard_map/all_gather | solution.py:15
  309.6 16.0 %while.39 = (s32[]{:T(128)}, f32[8,64,128]{2,1,0:T(8,128)S(1)}, s32[]{:T(128)}, bf16[16,8]{1,0:T(8,128)(2,1)S(1)}, bf16[16,8,64,128]{3,2,1,0:T(8,128)(2,1)}, /*index=5*/s32[]{:T(128)}, s32[]{:T(128)}, s32[]{:T(128)}) while((s32[]{:T(128)}, f32[8,64,128]{2,1,0:T(8,128)S(1)}, s32[]{:T(128)}, bf16[16,8]{1,0:T(8,128)(2,1)S(1)}, ...), condition=%wide.region_9.10_spmd, body=%wide.region_8.9_spmd.sunk | while | flops 196621 | bytes 655567 | solution.py:29
  325.6 10.9 %fusion.29 = bf16[8,512,1,8,64]{1,4,3,0,2:T(8,128)(2,1)S(1)} fusion(f32[8,512,1,8,64]{1,4,3,2,0:T(8,128)} %get-tuple-element.123, f32[8,512,1,8,64]{1,0,4,3,2:T(8,128)} %reshape.178, f32[8]{0:T(128)S(1)} %dynamic_slice.44, f32[8,512,8]{1,2,0:T(8,128)S(1)} %get-tuple-element.260, bf16[8,512,128,1]{2,1,3,0:T(8,128)(2,1)S(1)} %bitcast.137, ...), kind=kOutput, calls=%fused_computation.40 | convolution fusion | flops 548929536 | bytes 24510752 | tf_op jit(solution)/shard_map/cign,cghpn->cighp/dot_general | solution.py:116
  341.0 7.1 %all_to_all.50 = bf16[16,256,512]{1,0,2:T(8,128)(2,1)} reshape(bf16[8,512,1,8,64]{1,0,4,3,2:T(8,128)(2,1)} %copy.89) | data formatting | bytes 8388608 | tf_op jit(solution)/shard_map/all_to_all | solution.py:124
  351.8 57.4 %all_to_all.58 = bf16[16,256,512]{1,2,0:T(8,128)(2,1)} all-to-all(bf16[16,256,512]{1,2,0:T(8,128)(2,1)S(1)} %copy.90), channel_id=1, replica_groups=mesh['seq'=16,'head'=16] {'head'}, dimensions={0} | all-to-all | bytes 8388608 | tf_op jit(solution)/shard_map/all_to_all | solution.py:124
  409.2 6.3 %copy.91 = bf16[256,8192]{1,0:T(8,128)(2,1)} copy(bf16[256,8192]{0,1:T(8,128)(2,1)} %bitcast.135) | data formatting | bytes 8388608 | tf_op jit(solution)/shard_map/all_to_all | solution.py:124
  (149 shorter events, 90.3 us)
Async XLA Ops:
  6.5 137.8 %all-gather.6.cloned.1.call-start = ((), (), s32[]{:S(2)}) async-start(), calls=%async_computation.4 | async-start | bytes 8912896 | tf_op jit(solution)/shard_map/all_gather | solution.py:51
  7.3 192.4 %all-gather.8.cloned.1.call-start = ((), (), s32[]{:S(2)}) async-start(), calls=%async_computation.5 | async-start | bytes 8912896 | tf_op jit(solution)/shard_map/all_gather | solution.py:50
  9.6 13.3 %all-to-all-start.2 = ((bf16[256,16,8]{0,2,1:T(8,128)(2,1)}), bf16[256,16,8]{0,2,1:T(8,128)(2,1)S(1)}, u32[]{:S(2)}, u32[]{:S(2)}) async-start(bf16[256,16,8]{0,2,1:T(8,128)(2,1)} %bitcast.102), calls=%async_computation.2 | async-start | bytes 131072 | tf_op jit(solution)/shard_map/all_to_all | solution.py:45
  22.9 10.3 %all-to-all-start.1 = ((bf16[256,16,8]{0,2,1:T(8,128)(2,1)}), bf16[256,16,8]{0,2,1:T(8,128)(2,1)S(1)}, u32[]{:S(2)}, u32[]{:S(2)}) async-start(bf16[256,16,8]{0,2,1:T(8,128)(2,1)} %bitcast.103), calls=%async_computation.1 | async-start | bytes 131072 | tf_op jit(solution)/shard_map/all_to_all | solution.py:42
  33.2 81.6 %all-to-all-start = ((bf16[256,16,512]{0,2,1:T(8,128)(2,1)}), bf16[256,16,512]{0,2,1:T(8,128)(2,1)}, u32[]{:S(2)}, u32[]{:S(2)}) async-start(bf16[256,16,512]{0,2,1:T(8,128)(2,1)} %bitcast.134), calls=%async_computation | async-start | bytes 8388608 | tf_op jit(solution)/shard_map/all_to_all | solution.py:40
  39.5 270.1 %all-gather.10.cloned.1.call-start = ((), (), s32[]{:S(2)}) async-start(), calls=%async_computation.6 | async-start | bytes 2228224 | tf_op jit(solution)/shard_map/all_gather | solution.py:15
  261.6 9.9 %copy-start.1 = (u32[256]{0:T(256)S(1)}, u32[256]{0:T(256)}, u32[]{:S(2)}) copy-start(u32[256]{0:T(256)} %constant.87) | copy-start | bytes 3076
  261.6 11.1 %copy-start = (f32[128]{0:T(128)S(1)}, f32[128]{0:T(128)}, u32[]{:S(2)}) copy-start(f32[128]{0:T(128)} %param.17) | copy-start | bytes 1540
Sparse Core Ops, SparseCore 0:
  9.8 115.7 all-gather.5
  128.0 71.6 all-gather.7
  271.6 37.8 all-gather.9
where the time goes:
time: 424 us; the launch traced here: 422 us
  waiting for transfers between devices  138 us (33%)
  blocking collectives  81.1 us (19%)
  matrix products  66.9 us (16%)
  local copies, waits for them, and re-layouts  60.3 us (14%)
  other arithmetic  43.7 us (10%)
  starting transfers between devices  16.6 us (4%)
  between operations  14 us (3%)
    all_to_all x1, waiting for transfers between devices, shards(): lax.all_to_all(features, 'head', split_axis=1, concat_axis=0, tiled=True)  65.2 us
    all_to_all x1, blocking collectives, shards(): lax.all_to_all(mixed_rows, 'head', split_axis=0, concat_axis=1, tiled=True)  57.4 us
    all_gather x1, waiting for transfers between devices, shards(): lax.all_gather(inject, 'head', axis=0, tiled=True)  54.1 us
    dot_general x8, matrix products, span_terms(): jnp.einsum('ghij,jghp->ighp', weights, drive_c, preferred_element_type=jn...  37.3 us
    unnamed x1, blocking collectives  23.8 us
    convert_element_type x2, local copies, waits for them, and re-layouts, shards(): regrouped.reshape(seq_rows, local_heads, HEAD_DIM).astype(jnp.float32)  17.9 us
    all_to_all x3, local copies, waits for them, and re-layouts, shards(): lax.all_to_all(mixed_rows, 'head', split_axis=0, concat_axis=1, tiled=True)  17.1 us
    dot_general x8, matrix products, span_terms(): jnp.einsum('jghp,jgn->ghpn', scaled, inject_c, preferred_element_type=jnp...  16.4 us
  transfers between devices with their start and end apart: 6, of which 5 were waited for; matrix products, arithmetic and copies ran while one was open for 12% of the time, Pallas kernels for 0%

commit v1 on v0

--- a/solution.py
+++ b/solution.py
@@ -47,7 +47,9 @@
         ).astype(log_decay.dtype),
     )
     inject_all, readout_all = (
-        lax.all_gather(inject, "head", axis=0, tiled=True),
+        jnp.concatenate(
+            lax.all_to_all(jnp.stack([inject] * lax.axis_size("head")), "head", 0, 0), axis=0
+        ),
         lax.all_gather(readout, "head", axis=0, tiled=True),
     )
     first_col = head_index * local_heads // group_heads * STATE

time: 424 us -> 457 us (1.078)
  blocking collectives: 81.1 us -> 170 us
  waiting for transfers between devices: 138 us -> 77.6 us
    all_to_all x0 -> x1, blocking collectives: none -> 84 us  [shards(): lax.all_to_all(features, 'head', split_axis=1, concat_axis=0, tiled=True)]
    all_gather x1 -> x0, waiting for transfers between devices: 54.1 us -> none  [shards(): lax.all_gather(inject, 'head', axis=0, tiled=True)]
    all_to_all x1, waiting for transfers between devices: 65.2 us -> 58 us  [shards(): lax.all_to_all(jnp.stack([inject] * lax.axis_size('head')), 'head', 0, 0)]
    unnamed x1, blocking collectives: 23.8 us -> 28.7 us
    unnamed x11 -> x13, local copies, waits for them, and re-layouts: 14.1 us -> 14.2 us
  transfers between devices with their start and end apart: 6 -> 5, of which waited for: 5 -> 4; matrix products, arithmetic and copies ran while one was open for 12% -> 12% of each run, Pallas kernels for 0% -> 0%
where the time goes in v1:
time: 457 us; the launch traced here: 455 us
  blocking collectives  170 us (37%)
  waiting for transfers between devices  77.6 us (17%)
  matrix products  67.2 us (15%)
  local copies, waits for them, and re-layouts  64.8 us (14%)
  other arithmetic  43.2 us (9%)
  starting transfers between devices  16.2 us (4%)
  between operations  14.3 us (3%)
    all_to_all x1, blocking collectives, shards(): lax.all_to_all(features, 'head', split_axis=1, concat_axis=0, tiled=True)  84 us
    all_to_all x1, waiting for transfers between devices, shards(): lax.all_to_all(jnp.stack([inject] * lax.axis_size('head')), 'head', 0, 0)  58 us
    all_to_all x1, blocking collectives, shards(): lax.all_to_all(mixed_rows, 'head', split_axis=0, concat_axis=1, tiled=True)  57.6 us
    dot_general x8, matrix products, span_terms(): jnp.einsum('ghij,jghp->ighp', weights, drive_c, preferred_element_type=jn...  37.4 us
    unnamed x1, blocking collectives  28.7 us
    convert_element_type x2, local copies, waits for them, and re-layouts, shards(): regrouped.reshape(seq_rows, local_heads, HEAD_DIM).astype(jnp.float32)  17.9 us
    all_to_all x3, local copies, waits for them, and re-layouts, shards(): lax.all_to_all(mixed_rows, 'head', split_axis=0, concat_axis=1, tiled=True)  17.1 us
    dot_general x8, matrix products, span_terms(): jnp.einsum('jghp,jgn->ghpn', scaled, inject_c, preferred_element_type=jnp...  16.6 us
  transfers between devices with their start and end apart: 5, of which 4 were waited for; matrix products, arithmetic and copies ran while one was open for 12% of the time, Pallas kernels for 0%

profile of v1, /device:TPU:225, one launch (start us, length us, event | category | flops | bytes accessed | tf_op | source)
XLA Modules:
  0.0 454.5 jit_solution(6791503861876137452)
XLA Ops:
  8.9 6.8 %all-to-all-start.2 = ((bf16[256,16,8]{0,2,1:T(8,128)(2,1)}), bf16[256,16,8]{0,2,1:T(8,128)(2,1)S(1)}, u32[]{:S(2)}, u32[]{:S(2)}) async-start(bf16[256,16,8]{0,2,1:T(8,128)(2,1)} %bitcast.103), calls=%async_computation.2 | async-start | bytes 131072 | tf_op jit(solution)/shard_map/all_to_all | solution.py:45
  17.3 4.9 %all-to-all-done.2 = bf16[256,16,8]{0,2,1:T(8,128)(2,1)S(1)} async-done(((bf16[256,16,8]{0,2,1:T(8,128)(2,1)}), bf16[256,16,8]{0,2,1:T(8,128)(2,1)S(1)}, u32[]{:S(2)}, u32[]{:S(2)}) %all-to-all-start.2) | async-done | bytes 65568 | tf_op jit(solution)/shard_map/all_to_all | solution.py:45
  25.7 6.4 %copy.78 = bf16[256,8192]{0,1:T(8,128)(2,1)} copy(bf16[256,8192]{1,0:T(8,128)(2,1)} %param.12) | data formatting | bytes 8388608 | tf_op args[0]
  32.5 84.0 %all_to_all.63 = bf16[256,16,512]{0,2,1:T(8,128)(2,1)} all-to-all(bf16[256,16,512]{0,2,1:T(8,128)(2,1)} %bitcast.135), channel_id=1, replica_groups=mesh['seq'=16,'head'=16] {'head'}, dimensions={1} | all-to-all | bytes 8388608 | tf_op jit(solution)/shard_map/all_to_all | solution.py:40
  120.8 5.9 %all-to-all-start.3 = ((bf16[16,256,1024]{2,1,0:T(8,128)(2,1)}), bf16[16,256,1024]{2,1,0:T(8,128)(2,1)}, u32[]{:S(2)}, u32[]{:S(2)}) async-start(bf16[16,256,1024]{2,1,0:T(8,128)(2,1)} %stack.2), calls=%async_computation.3 | async-start | bytes 16777216 | tf_op jit(solution)/shard_map/all_to_all | solution.py:51
  126.8 9.0 %reduce-window.6 = f32[8,8,4,128]{3,1,2,0:T(8,128)S(1)} reduce-window(f32[8,8,4,128]{3,1,2,0:T(8,128)S(1)} %bitcast.140, f32[]{:T(128)} %constant.75.clone.1), window={size=1x1x1x128 pad=0_0x0_0x0_0x127_0}, to_apply=%region_0.1 | reduce-window | flops 4161536 | bytes 262148 | tf_op jit(solution)/shard_map/reduce-window
  139.8 8.0 %copy.79 = f32[16,256,512]{1,0,2:T(8,128)} copy(f32[16,256,512]{1,2,0:T(8,128)S(1)} %convert_bitcast_fusion) | data formatting | bytes 16777216 | tf_op jit(solution)/shard_map/convert_element_type | solution.py:61
  147.9 9.8 %reshape.184 = f32[8,512,1,8,64]{1,0,4,3,2:T(8,128)} reshape(f32[16,256,512]{1,0,2:T(8,128)} %copy.79) | data formatting | bytes 16777216 | tf_op jit(solution)/shard_map/convert_element_type | solution.py:61
  165.9 58.0 %all-to-all-done.3 = bf16[16,256,1024]{2,1,0:T(8,128)(2,1)} async-done(((bf16[16,256,1024]{2,1,0:T(8,128)(2,1)}), bf16[16,256,1024]{2,1,0:T(8,128)(2,1)}, u32[]{:S(2)}, u32[]{:S(2)}) %all-to-all-start.3) | async-done | bytes 8388640 | tf_op jit(solution)/shard_map/all_to_all | solution.py:51
  228.1 59.3 %while.40 = (s32[]{:T(128)}, f32[8,512,1,8,64]{1,4,3,2,0:T(8,128)}, f32[8,8,64,128]{3,2,1,0:T(8,128)}, bf16[8,512,1,8,64]{1,4,3,2,0:T(8,128)(2,1)}, f32[8,512,8]...) while((s32[]{:T(128)}, f32[8,512,1,8,64]{1,4,3,2,0:T(8,128)}, ...), condition=%wide.region_3.4_spmd.clone.clone, body=%wide.region_2.3_spmd.clone.clone.sunk | while | flops 414191616 | bytes 5492413 | solution.py:94
  228.5 4.7 %fusion.52 = f32[8,512,1,8,64]{1,4,3,2,0:T(8,128)} fusion(f32[8,512,1,8,64]{1,4,3,2,0:T(8,128)} %get-tuple-element.377, s32[]{:T(128)} %get-tuple-element.376, f32[512,512]{1,0:T(8,128)S(1)} %fusion.51, f32[8,512]{1,0:T(8,128)S(1)} %dynamic-slice_bitcast_fusion.2, pred[512,512]{1,0:T(8,128)(4,1)S(1)} %iota_compare_fusion.2, ...), kind=kOutput, calls=%fused_computation.12.clone.1 | convolution fusion | flops 278921216 | bytes 2917376 | tf_op jit(solution)/shard_map/while/body/eval_jaxpr/ghij,jghp->ighp/dot_general | solution.py:83
  235.9 4.7 %fusion.52 = f32[8,512,1,8,64]{1,4,3,2,0:T(8,128)} fusion(f32[8,512,1,8,64]{1,4,3,2,0:T(8,128)} %get-tuple-element.377, s32[]{:T(128)} %get-tuple-element.376, f32[512,512]{1,0:T(8,128)S(1)} %fusion.51, f32[8,512]{1,0:T(8,128)S(1)} %dynamic-slice_bitcast_fusion.2, pred[512,512]{1,0:T(8,128)(4,1)S(1)} %iota_compare_fusion.2, ...), kind=kOutput, calls=%fused_computation.12.clone.1 | convolution fusion | flops 278921216 | bytes 2917376 | tf_op jit(solution)/shard_map/while/body/eval_jaxpr/ghij,jghp->ighp/dot_general | solution.py:83
  243.3 4.7 %fusion.52 = f32[8,512,1,8,64]{1,4,3,2,0:T(8,128)} fusion(f32[8,512,1,8,64]{1,4,3,2,0:T(8,128)} %get-tuple-element.377, s32[]{:T(128)} %get-tuple-element.376, f32[512,512]{1,0:T(8,128)S(1)} %fusion.51, f32[8,512]{1,0:T(8,128)S(1)} %dynamic-slice_bitcast_fusion.2, pred[512,512]{1,0:T(8,128)(4,1)S(1)} %iota_compare_fusion.2, ...), kind=kOutput, calls=%fused_computation.12.clone.1 | convolution fusion | flops 278921216 | bytes 2917376 | tf_op jit(solution)/shard_map/while/body/eval_jaxpr/ghij,jghp->ighp/dot_general | solution.py:83
  258.2 4.7 %fusion.52 = f32[8,512,1,8,64]{1,4,3,2,0:T(8,128)} fusion(f32[8,512,1,8,64]{1,4,3,2,0:T(8,128)} %get-tuple-element.377, s32[]{:T(128)} %get-tuple-element.376, f32[512,512]{1,0:T(8,128)S(1)} %fusion.51, f32[8,512]{1,0:T(8,128)S(1)} %dynamic-slice_bitcast_fusion.2, pred[512,512]{1,0:T(8,128)(4,1)S(1)} %iota_compare_fusion.2, ...), kind=kOutput, calls=%fused_computation.12.clone.1 | convolution fusion | flops 278921216 | bytes 2917376 | tf_op jit(solution)/shard_map/while/body/eval_jaxpr/ghij,jghp->ighp/dot_general | solution.py:83
  265.6 4.7 %fusion.52 = f32[8,512,1,8,64]{1,4,3,2,0:T(8,128)} fusion(f32[8,512,1,8,64]{1,4,3,2,0:T(8,128)} %get-tuple-element.377, s32[]{:T(128)} %get-tuple-element.376, f32[512,512]{1,0:T(8,128)S(1)} %fusion.51, f32[8,512]{1,0:T(8,128)S(1)} %dynamic-slice_bitcast_fusion.2, pred[512,512]{1,0:T(8,128)(4,1)S(1)} %iota_compare_fusion.2, ...), kind=kOutput, calls=%fused_computation.12.clone.1 | convolution fusion | flops 278921216 | bytes 2917376 | tf_op jit(solution)/shard_map/while/body/eval_jaxpr/ghij,jghp->ighp/dot_general | solution.py:83
  273.0 4.7 %fusion.52 = f32[8,512,1,8,64]{1,4,3,2,0:T(8,128)} fusion(f32[8,512,1,8,64]{1,4,3,2,0:T(8,128)} %get-tuple-element.377, s32[]{:T(128)} %get-tuple-element.376, f32[512,512]{1,0:T(8,128)S(1)} %fusion.51, f32[8,512]{1,0:T(8,128)S(1)} %dynamic-slice_bitcast_fusion.2, pred[512,512]{1,0:T(8,128)(4,1)S(1)} %iota_compare_fusion.2, ...), kind=kOutput, calls=%fused_computation.12.clone.1 | convolution fusion | flops 278921216 | bytes 2917376 | tf_op jit(solution)/shard_map/while/body/eval_jaxpr/ghij,jghp->ighp/dot_general | solution.py:83
  287.6 8.9 %while.41 = (s32[]{:T(128)}, f32[8,64,128]{2,1,0:T(8,128)S(1)}, f32[8,8,64,128]{3,2,1,0:T(8,128)S(1)}, f32[8,8]{1,0:T(8,128)S(1)}, f32[8,8,64,128]{3,2,1,0:T(8,128)}, /*index=5*/s32[]{:T(128)}, s32[]{:T(128)}) while((s32[]{:T(128)}, f32[8,64,128]{2,1,0:T(8,128)S(1)}, f32[8,8,64,128]{3,2,1,0:T(8,128)S(1)}, f32[8,8]{1,0:T(8,128)S(1)}, ...), condition=%wide.region_5.6_spmd.clone, body=%wide.region_4.5_spmd.clone.sunk | while | flops 262147 | bytes 1310916 | solution.py:103
  299.1 28.7 %all-reduce = bf16[128]{0:T(256)(128)(2,1)S(1)} all-reduce(bf16[128]{0:T(256)(128)(2,1)S(1)} %dynamic-update-slice), channel_id=2, replica_groups=mesh['seq'=16,'head'=16] {'seq'}, use_global_device_ids=true, to_apply=%add | all-reduce | flops 128 | bytes 512
  327.9 13.5 %all-gather.7.cloned.1.call-done = bf16[128,64,128]{2,1,0:T(8,128)(2,1)} async-done(((bf16[8,64,128]{2,1,0:T(8,128)(2,1)}), bf16[128,64,128]{2,1,0:T(8,128)(2,1)}) %all-gather.7.cloned.1.call-update) | async-done | bytes 2097168 | tf_op jit(solution)/shard_map/all_gather | solution.py:15
  341.5 16.0 %while.39 = (s32[]{:T(128)}, f32[8,64,128]{2,1,0:T(8,128)S(1)}, s32[]{:T(128)}, bf16[16,8]{1,0:T(8,128)(2,1)S(1)}, bf16[16,8,64,128]{3,2,1,0:T(8,128)(2,1)}, /*index=5*/s32[]{:T(128)}, s32[]{:T(128)}, s32[]{:T(128)}) while((s32[]{:T(128)}, f32[8,64,128]{2,1,0:T(8,128)S(1)}, s32[]{:T(128)}, bf16[16,8]{1,0:T(8,128)(2,1)S(1)}, ...), condition=%wide.region_9.10_spmd, body=%wide.region_8.9_spmd.sunk | while | flops 196621 | bytes 655567 | solution.py:29
  357.5 10.9 %fusion.29 = bf16[8,512,1,8,64]{1,4,3,0,2:T(8,128)(2,1)S(1)} fusion(f32[8,512,1,8,64]{1,4,3,2,0:T(8,128)} %get-tuple-element.123, f32[8,512,1,8,64]{1,0,4,3,2:T(8,128)} %reshape.184, f32[8]{0:T(128)S(1)} %dynamic_slice.44, f32[8,512,8]{1,2,0:T(8,128)S(1)} %get-tuple-element.260, bf16[8,512,128,1]{2,1,3,0:T(8,128)(2,1)S(1)} %bitcast.138, ...), kind=kOutput, calls=%fused_computation.40 | convolution fusion | flops 548929536 | bytes 24510752 | tf_op jit(solution)/shard_map/cign,cghpn->cighp/dot_general | solution.py:118
  373.0 7.1 %all_to_all.54 = bf16[16,256,512]{1,0,2:T(8,128)(2,1)} reshape(bf16[8,512,1,8,64]{1,0,4,3,2:T(8,128)(2,1)} %copy.89) | data formatting | bytes 8388608 | tf_op jit(solution)/shard_map/all_to_all | solution.py:126
  383.7 57.6 %all_to_all.64 = bf16[16,256,512]{1,2,0:T(8,128)(2,1)} all-to-all(bf16[16,256,512]{1,2,0:T(8,128)(2,1)S(1)} %copy.90), channel_id=1, replica_groups=mesh['seq'=16,'head'=16] {'head'}, dimensions={0} | all-to-all | bytes 8388608 | tf_op jit(solution)/shard_map/all_to_all | solution.py:126
  441.3 6.3 %copy.91 = bf16[256,8192]{1,0:T(8,128)(2,1)} copy(bf16[256,8192]{0,1:T(8,128)(2,1)} %bitcast.136) | data formatting | bytes 8388608 | tf_op jit(solution)/shard_map/all_to_all | solution.py:126
  (150 shorter events, 94.2 us)
Async XLA Ops:
  6.5 218.6 %all-gather.5.cloned.1.call-start = ((), (), s32[]{:S(2)}) async-start(), calls=%async_computation.5 | async-start | bytes 8912896 | tf_op jit(solution)/shard_map/all_gather | solution.py:53
  8.9 13.3 %all-to-all-start.2 = ((bf16[256,16,8]{0,2,1:T(8,128)(2,1)}), bf16[256,16,8]{0,2,1:T(8,128)(2,1)S(1)}, u32[]{:S(2)}, u32[]{:S(2)}) async-start(bf16[256,16,8]{0,2,1:T(8,128)(2,1)} %bitcast.103), calls=%async_computation.2 | async-start | bytes 131072 | tf_op jit(solution)/shard_map/all_to_all | solution.py:45
  22.2 10.3 %all-to-all-start.1 = ((bf16[256,16,8]{0,2,1:T(8,128)(2,1)}), bf16[256,16,8]{0,2,1:T(8,128)(2,1)S(1)}, u32[]{:S(2)}, u32[]{:S(2)}) async-start(bf16[256,16,8]{0,2,1:T(8,128)(2,1)} %bitcast.104), calls=%async_computation.1 | async-start | bytes 131072 | tf_op jit(solution)/shard_map/all_to_all | solution.py:42
  32.5 84.0 %copy-start = (bf16[256,1024]{1,0:T(8,128)(2,1)S(1)}, bf16[256,1024]{1,0:T(8,128)(2,1)}, u32[]{:S(2)}) copy-start(bf16[256,1024]{1,0:T(8,128)(2,1)} %param.15) | copy-start | bytes 1572868
  120.8 103.0 %all-to-all-start.3 = ((bf16[16,256,1024]{2,1,0:T(8,128)(2,1)}), bf16[16,256,1024]{2,1,0:T(8,128)(2,1)}, u32[]{:S(2)}, u32[]{:S(2)}) async-start(bf16[16,256,1024]{2,1,0:T(8,128)(2,1)} %stack.2), calls=%async_computation.3 | async-start | bytes 16777216 | tf_op jit(solution)/shard_map/all_to_all | solution.py:51
  126.7 214.8 %all-gather.7.cloned.1.call-start = ((), (), s32[]{:S(2)}) async-start(), calls=%async_computation.6 | async-start | bytes 2228224 | tf_op jit(solution)/shard_map/all_gather | solution.py:15
  287.4 9.9 %copy-start.2 = (u32[256]{0:T(256)S(1)}, u32[256]{0:T(256)}, u32[]{:S(2)}) copy-start(u32[256]{0:T(256)} %constant.87) | copy-start | bytes 3076
  287.4 11.2 %copy-start.1 = (f32[128]{0:T(128)S(1)}, f32[128]{0:T(128)}, u32[]{:S(2)}) copy-start(f32[128]{0:T(128)} %param.17) | copy-start | bytes 1540
Sparse Core Ops, SparseCore 0:
  9.8 111.3 all-gather.4
  297.4 44.0 all-gather.6
